TPU v7x, 768 devices: a whole 4x8x12 slice. The times are simulated.
768 devices in a mesh: gz: 32 (over x, z_lo, core), ch: 24 (over z_hi, y).
Axes of the slice: x: 4, y: 8, z: 12 (z_hi: 3, z_lo: 4; z = z_hi * 4 + z_lo), core: 2. Of those that a mesh axis runs over, the one named last changes fastest.
Arguments:
- inputs: bfloat16 [64, 192, 6144], P('gz', 'ch'), may hold values from -6 to 6
- out_grad: bfloat16 [64, 192, 6144], P('gz', 'ch'), may hold values from -6 to 6
- filters: bfloat16 [864, 32], replicated, may hold values from -0.21875 to 0.21875
Outputs:
- in_grad: bfloat16 [64, 192, 6144], P('gz', 'ch')
- filter_grad: float32 [864, 32], replicated
All inputs are finite; a program needn't handle non-finite values.
Results may differ from a plain program's by a relative error of at most 0.001.
Values may be sent and summed in bfloat16 or wider, within the bound.
A program may use at most 32 MiB of HBM per device.

v0:
```python
import jax
import jax.numpy as jnp
from jax import lax
from jax.sharding import PartitionSpec as P


def extended(block, sides, width):
    for axis, dim in sides:
        count = lax.axis_size(axis)
        forward = [(i, i + 1) for i in range(count - 1)]
        forward.append((count - 1, 0))
        backward = [(target, source) for source, target in forward]
        low = lax.ppermute(
            lax.slice_in_dim(block, block.shape[dim] - width, None, axis=dim), axis, forward
        )
        high = lax.ppermute(lax.slice_in_dim(block, 0, width, axis=dim), axis, backward)
        block = jnp.concatenate([low, block, high], axis=dim)
    return block


def per_device(inputs, out_grad, filters):
    depth, rows, width = inputs.shape
    chans = filters.shape[1]
    length = width // chans
    padded = extended(out_grad, (("gz", 0), ("ch", 1)), 1)
    grid = padded.reshape(depth + 2, rows + 2, length, chans)
    shifted = jnp.concatenate([jnp.roll(grid, kx - 1, axis=2) for kx in range(3)], axis=-1)
    values = inputs.reshape(depth * rows * length, chans)
    accum = jnp.zeros((depth * rows * length, chans), jnp.float32)
    pieces = []
    for kz in range(3):
        for ky in range(3):
            window = shifted[2 - kz : 2 - kz + depth, 2 - ky : 2 - ky + rows]
            window = window.reshape(depth * rows * length, 3 * chans)
            pair = kz * 3 + ky
            block = filters[pair * 3 * chans : (pair + 1) * 3 * chans].reshape(3, chans, chans)
            turned = jnp.transpose(block, (0, 2, 1)).reshape(3 * chans, chans)
            accum = accum + jnp.dot(window, turned, preferred_element_type=jnp.float32)
            local_part = lax.dot_general(
                values, window, (((0,), (0,)), ((), ())), preferred_element_type=jnp.float32
            )
            local_part = jnp.transpose(local_part.reshape(chans, 3, chans), (1, 0, 2)).reshape(
                3 * chans, chans
            )
            pieces.append(local_part)
    in_grad = accum.astype(jnp.bfloat16).reshape(depth, rows, width)
    local_sum = jnp.concatenate(pieces, axis=0)
    total = lax.psum(local_sum, ("gz", "ch"))
    count = depth * rows * length * lax.axis_size("gz") * lax.axis_size("ch")
    scale = jnp.float32(1.0) / jnp.sqrt(jnp.float32(count))
    return (in_grad, total * scale)


def solution(mesh):
    placed = (P("gz", "ch", None), P("gz", "ch", None), P())
    return jax.shard_map(
        per_device,
        mesh=mesh,
        in_specs=placed,
        out_specs=(P("gz", "ch", None), P()),
        check_vma=False,
    )
```

profile of v0, /device:TPU:1, one launch (start us, length us, event | category | flops | bytes accessed | tf_op | source)
XLA Modules:
  0.0 574.8 jit_solution(309501567765805526)
XLA Ops:
  7.2 1.0 fusion.5
  8.2 5.4 collective-permute-start
  13.6 8.9 %collective-permute-start.1 = (bf16[1,8,6144]{2,1,0:T(8,128)(2,1)S(1)}, bf16[1,8,6144]{2,1,0:T(8,128)(2,1)S(1)}, u32[]{:S(2)}, u32[]{:S(2)}) collective-permute-start(bf16[1,8,6144]{2,1,0:T(8,128)(2,1)S(1)} %get-tuple-element.17), channel_id=1, source_target_pairs={{24,0},{48,24},{72,48},{96,72},{120,96},{144,120},{168,144},{192,1... | collective-permute-start | bytes 294920 | tf_op jit(solution)/shard_map/ppermute | solution.py:16
  22.5 0.9 constant_dynamic-update-slice_fusion.1
  23.6 1.9 collective-permute-start.2
  25.6 12.7 %collective-permute-start.3 = (bf16[4,1,6144]{2,1,0:T(2,128)(2,1)S(1)}, bf16[4,1,6144]{2,1,0:T(2,128)(2,1)S(1)}, u32[]{:S(2)}, u32[]{:S(2)}) collective-permute-start(bf16[4,1,6144]{2,1,0:T(2,128)(2,1)S(1)} %get-tuple-element.16), channel_id=1, source_target_pairs={{1,0},{2,1},{3,2},{4,3},{5,4},{6,5},{7,6},{8,7},{9,8},{10,9},{11,1... | collective-permute-start | bytes 147464 | tf_op jit(solution)/shard_map/ppermute | solution.py:16
  38.2 0.9 fusion.6
  39.2 1.5 reshape.177
  43.3 0.4 pad_maximum_fusion
  43.6 0.4 copy.98
  44.0 1.3 reshape.148
  45.3 1.1 fusion.2
  46.5 2.2 maximum_maximum_fusion
  48.7 3.0 fusion.1
  51.7 2.1 copy.99
  53.8 1.9 reshape.149
  55.7 0.4 convolution_bitcast_fusion.8
  56.4 3.1 copy.101
  59.5 1.9 reshape.152
  61.4 0.4 convolution_bitcast_fusion.7
  62.1 2.1 copy.103
  64.2 2.1 reshape.155
  66.3 0.4 convolution_bitcast_fusion.6
  67.0 3.1 copy.105
  70.1 1.9 reshape.158
  72.0 0.4 convolution_bitcast_fusion.5
  72.7 3.0 copy.107
  75.8 2.6 reshape.161
  78.3 1.4 convolution_bitcast_fusion.4
  80.1 3.0 copy.109
  83.1 1.9 reshape.164
  85.1 0.4 convolution_bitcast_fusion.3
  85.7 3.0 copy.111
  88.8 2.6 reshape.167
  91.3 1.4 convolution_bitcast_fusion.2
  93.1 3.0 copy.113
  96.1 2.2 reshape.170
  98.3 0.4 convolution_bitcast_fusion.1
  99.2 3.1 copy.115
  102.2 1.9 reshape.173
  104.2 0.4 convolution_bitcast_fusion
  104.8 0.7 concatenate.25
  106.3 0.4 copy-done.1
  107.4 0.4 copy-done.5
  108.5 0.4 copy.117
  108.9 1.5 reshape.176
  110.5 455.9 %all-reduce.2.cloned.1.call-done = f32[864,32]{0,1:T(8,128)} async-done(((f32[864,32]{0,1:T(8,128)}), f32[864,32]{0,1:T(8,128)}) %all-reduce.2.cloned.1.call-update) | async-done | bytes 110608 | tf_op jit(solution)/shard_map/psum | solution.py:48
  566.4 1.6 broadcast_multiply_fusion
  (87 shorter events, 7.8 us)
Async XLA Ops:
  7.2 559.2 %all-reduce.2.cloned.1.call-start = ((), (), s32[]{:S(2)}) async-start(), calls=%async_computation | async-start | bytes 229376 | tf_op jit(solution)/shard_map/psum | solution.py:48
  8.2 14.3 %collective-permute-start = (bf16[1,8,6144]{2,1,0:T(8,128)(2,1)S(1)}, bf16[1,8,6144]{2,1,0:T(8,128)(2,1)S(1)}, u32[]{:S(2)}, u32[]{:S(2)}) collective-permute-start(bf16[1,8,6144]{2,1,0:T(8,128)(2,1)S(1)} %get-tuple-element.18), channel_id=1, source_target_pairs={{0,24},{24,48},{48,72},{72,96},{96,120},{120,144},{144,168},{168,1... | collective-permute-start | bytes 294920 | tf_op jit(solution)/shard_map/ppermute | solution.py:13
  13.6 9.9 %collective-permute-start.1 = (bf16[1,8,6144]{2,1,0:T(8,128)(2,1)S(1)}, bf16[1,8,6144]{2,1,0:T(8,128)(2,1)S(1)}, u32[]{:S(2)}, u32[]{:S(2)}) collective-permute-start(bf16[1,8,6144]{2,1,0:T(8,128)(2,1)S(1)} %get-tuple-element.17), channel_id=1, source_target_pairs={{24,0},{48,24},{72,48},{96,72},{120,96},{144,120},{168,144},{192,1... | collective-permute-start | bytes 294920 | tf_op jit(solution)/shard_map/ppermute | solution.py:16
  23.6 19.6 %collective-permute-start.2 = (bf16[4,1,6144]{2,1,0:T(2,128)(2,1)S(1)}, bf16[4,1,6144]{2,1,0:T(2,128)(2,1)S(1)}, u32[]{:S(2)}, u32[]{:S(2)}) collective-permute-start(bf16[4,1,6144]{2,1,0:T(2,128)(2,1)S(1)} %get-tuple-element.15), channel_id=1, source_target_pairs={{0,1},{1,2},{2,3},{3,4},{4,5},{5,6},{6,7},{7,8},{8,9},{9,10},{10,1... | collective-permute-start | bytes 147464 | tf_op jit(solution)/shard_map/ppermute | solution.py:13
  25.6 17.7 %collective-permute-start.3 = (bf16[4,1,6144]{2,1,0:T(2,128)(2,1)S(1)}, bf16[4,1,6144]{2,1,0:T(2,128)(2,1)S(1)}, u32[]{:S(2)}, u32[]{:S(2)}) collective-permute-start(bf16[4,1,6144]{2,1,0:T(2,128)(2,1)S(1)} %get-tuple-element.16), channel_id=1, source_target_pairs={{1,0},{2,1},{3,2},{4,3},{5,4},{6,5},{7,6},{8,7},{9,8},{10,9},{11,1... | collective-permute-start | bytes 147464 | tf_op jit(solution)/shard_map/ppermute | solution.py:16
  72.0 6.3 %copy-start = (bf16[3072,96]{0,1:T(8,128)(2,1)}, bf16[3072,96]{0,1:T(8,128)(2,1)S(1)}, u32[]{:S(2)}) copy-start(bf16[3072,96]{0,1:T(8,128)(2,1)S(1)} %reshape.158) | copy-start | bytes 1769476
  85.0 6.3 %copy-start.3 = (bf16[3072,96]{0,1:T(8,128)(2,1)}, bf16[3072,96]{0,1:T(8,128)(2,1)S(1)}, u32[]{:S(2)}) copy-start(bf16[3072,96]{0,1:T(8,128)(2,1)S(1)} %reshape.164) | copy-start | bytes 1769476
  98.3 0.8 copy-start.6
  105.6 1.1 copy-start.1
  105.8 1.1 copy-start.2
  106.1 1.2 copy-start.4
  106.7 1.2 copy-start.5
  106.9 1.2 copy-start.7
Sparse Core Ops, SparseCore 0:
  105.7 460.5 all-reduce.1
where the time goes:
time: 576 us; the launch traced here: 575 us
  waiting for transfers between devices  456 us (79%)
  local copies, waits for them, and re-layouts  63.9 us (11%)
  starting transfers between devices  28.9 us (5%)
  between operations  14.6 us (3%)
  matrix products  7.32 us (1%)
    psum x1, waiting for transfers between devices, per_device(): total = lax.psum(local_sum, ('gz', 'ch'))  456 us
    slice x10, local copies, waits for them, and re-layouts, per_device(): window = shifted[2 - kz:2 - kz + depth, 2 - ky:2 - ky + rows]  28.6 us
    ppermute x2, starting transfers between devices, extended(): lax.ppermute(lax.slice_in_dim(block, 0, width, axis=dim), axis, backward)  21.6 us
    reshape x9, local copies, waits for them, and re-layouts, per_device(): window = window.reshape(depth * rows * length, 3 * chans)  19.1 us
  transfers between devices with their start and end apart: 5, of which 1 were waited for; matrix products, arithmetic and copies ran while one was open for 2% of the time, Pallas kernels for 0%

commit v1 on v0

v1 whole, which is shorter than its diff:
```python
import functools

import jax
import jax.numpy as jnp
from jax import lax
from jax.experimental import pallas as pl
from jax.experimental.pallas import tpu as pltpu
from jax.sharding import PartitionSpec as P

MESH = pl.DeviceIdType.MESH
CH = 32
LANES = 128
PACK = LANES // CH
PIECES = 64
TAPS = 27


def kernel(
    geometry,
    scale,
    x_hbm,
    og_hbm,
    f_hbm,
    in_grad,
    filter_grad,
    x_v,
    og_v,
    f_v,
    rows32,
    edge,
    z_low,
    z_high,
    y_side,
    y_side32,
    tail,
    bands,
    xt,
    windows,
    grads,
    pieces,
    parts,
    layers,
    whole,
    local_sem,
    halo_send,
    halo_recv,
    ring_send,
    ring_recv,
):
    n_x, n_zlo, n_core, n_zhi, n_y = geometry
    depth, height, width = x_hbm.shape
    groups = width // LANES
    group_rows = depth * height
    n_gz, n_ch = n_x * n_zlo * n_core, n_zhi * n_y
    n_plane, n_z = n_x * n_y * n_core, n_zhi * n_zlo

    gz, ch = lax.axis_index("gz"), lax.axis_index("ch")
    core = lax.rem(gz, n_core)
    z_lo = lax.rem(gz // n_core, n_zlo)
    x = gz // (n_core * n_zlo)
    z_hi, y = ch // n_y, lax.rem(ch, n_y)
    rank = (x * n_y + y) * n_core + core
    z = z_hi * n_zlo + z_lo

    def plane_device(r):
        r_core, r_y, r_x = lax.rem(r, n_core), lax.rem(r // n_core, n_y), r // (n_core * n_y)
        return ((r_x * n_zlo + z_lo) * n_core + r_core, z_hi * n_y + r_y)

    def z_device(r):
        return ((x * n_zlo + lax.rem(r, n_zlo)) * n_core + core, (r // n_zlo) * n_y + y)

    up, down = lax.rem(gz + 1, n_gz), lax.rem(gz + n_gz - 1, n_gz)
    right, left = lax.rem(ch + 1, n_ch), lax.rem(ch + n_ch - 1, n_ch)
    neighbours = [(up, ch), (down, ch), (gz, right), (gz, left), (up, right), (down, right), (up, left), (down, left)]

    loads = [
        pltpu.make_async_copy(og_hbm, og_v, local_sem.at[0]),
        pltpu.make_async_copy(x_hbm, x_v, local_sem.at[1]),
        pltpu.make_async_copy(f_hbm, f_v, local_sem.at[2]),
    ]
    for load in loads:
        load.start()

    barrier = pltpu.get_barrier_semaphore()
    for device in neighbours:
        pl.semaphore_signal(barrier, inc=1, device_id=device, device_id_type=MESH)

    @pl.loop(1, n_z)
    def _(d):
        pl.semaphore_signal(barrier, inc=1, device_id=z_device(lax.rem(z + d, n_z)), device_id_type=MESH)

    @pl.loop(1, n_plane)
    def _(d):
        pl.semaphore_signal(
            barrier, inc=1, device_id=plane_device(lax.rem(rank + d, n_plane)), device_id_type=MESH
        )

    lane = lax.broadcasted_iota(jnp.int32, (height, LANES), 1) // CH
    row = lax.broadcasted_iota(jnp.int32, (height, LANES), 0)

    def tile(ref, layer, g):
        return ref[layer, :, g * LANES : (g + 1) * LANES].astype(jnp.float32)

    loads[0].wait()
    for layer in range(depth):
        for g in range(groups):
            block = tile(og_v, layer, g)
            rows32[layer, g : g + 1, :] = block[0:1]
            rows32[depth + layer, g : g + 1, :] = block[height - 1 : height]
    for k in range(2 * depth):
        edge[k] = rows32[k].astype(jnp.bfloat16)

    loads[2].wait()
    wide = lax.broadcasted_iota(jnp.int32, (CH, LANES), 1) // CH
    last = f_v.shape[1] // LANES
    tiles = [f_v[:, k * LANES : (k + 1) * LANES].astype(jnp.float32) for k in range(last)]
    tail[:, : f_v.shape[1] - last * LANES] = f_v[:, last * LANES :].astype(jnp.float32)
    tiles.append(tail[...])
    for w in range(9):
        place, turn = (3 * w) // PACK, (3 * w) % PACK
        slab = tiles[place]
        if turn:
            joined = slab if turn == 1 else jnp.where(wide >= turn, slab, tiles[place + 1])
            slab = pltpu.roll(joined, LANES - CH * turn, 1)
        for c_from in range(PACK):
            start = w * LANES + c_from * CH
            turn = (c_from - 1) % PACK
            band = pltpu.roll(slab, CH * turn, 1) if turn else slab
            used = wide != (c_from + 2) % PACK
            inside = used
            outside = jnp.zeros_like(band)
            if c_from == 0:
                inside = wide < 2
                outside = jnp.where(wide == PACK - 1, band, 0.0)
            elif c_from == PACK - 1:
                inside = wide >= 2
                outside = jnp.where(wide == 0, band, 0.0)
            bands[start : start + CH, :LANES] = jnp.where(inside, band, 0.0).astype(jnp.bfloat16)
            bands[start : start + CH, LANES:] = outside.astype(jnp.bfloat16)

    loads[1].wait()
    blocks = [jnp.concatenate([tile(x_v, layer, g) for layer in range(depth)], axis=0) for g in range(groups)]
    tall = lax.broadcasted_iota(jnp.int32, (group_rows, LANES), 1) // CH
    step = 8
    for g0 in range(0, groups, step):
        own = jnp.concatenate(blocks[g0 : g0 + step], axis=0)
        outer = jnp.concatenate(
            [
                jnp.where(tall < PACK // 2, blocks[(g + 1) % groups], blocks[(g - 1) % groups])
                for g in range(g0, g0 + step)
            ],
            axis=0,
        )
        columns = slice(g0 * group_rows, (g0 + step) * group_rows)
        xt[0:LANES, columns] = own.T.astype(jnp.bfloat16)
        xt[LANES : 2 * LANES, columns] = outer.T.astype(jnp.bfloat16)

    pl.semaphore_wait(barrier, len(neighbours) + (n_z - 1) + (n_plane - 1))

    halo = [
        (edge.at[pl.ds(depth, depth)], y_side.at[0, pl.ds(1, depth)]),
        (edge.at[pl.ds(0, depth)], y_side.at[1, pl.ds(1, depth)]),
        (edge.at[depth + depth - 1], y_side.at[0, 0]),
        (edge.at[depth], y_side.at[0, depth + 1]),
        (edge.at[depth - 1], y_side.at[1, 0]),
        (edge.at[0], y_side.at[1, depth + 1]),
    ]
    halo = [(og_v.at[depth - 1], z_low), (og_v.at[0], z_high)] + halo
    sends = [
        pltpu.make_async_remote_copy(
            src_ref=source,
            dst_ref=target,
            send_sem=halo_send.at[k],
            recv_sem=halo_recv.at[k],
            device_id=neighbours[k],
            device_id_type=MESH,
        )
        for k, (source, target) in enumerate(halo)
    ]
    for k in (4, 5, 6, 7, 2, 3, 0, 1):
        sends[k].start()
    for send in sends:
        send.wait_recv()

    for side in range(2):
        for layer in range(depth + 2):
            y_side32[side, layer] = y_side[side, layer].astype(jnp.float32)

    for g in range(groups):
        cut = slice(g * LANES, (g + 1) * LANES)
        planes = [z_low[:, cut].astype(jnp.float32)]
        planes += [tile(og_v, layer, g) for layer in range(depth)]
        planes += [z_high[:, cut].astype(jnp.float32)]
        moved = [[], planes, []]
        for layer, plane in enumerate(planes):
            low = jnp.broadcast_to(y_side32[0, layer, g : g + 1, :], plane.shape)
            high = jnp.broadcast_to(y_side32[1, layer, g : g + 1, :], plane.shape)
            moved[2].append(jnp.where(row == 0, low, pltpu.roll(plane, 1, 0)))
            moved[0].append(jnp.where(row == height - 1, high, pltpu.roll(plane, height - 1, 0)))
        for kz in range(3):
            for ky in range(3):
                w = 3 * kz + ky
                block = jnp.concatenate(moved[ky][2 - kz : 2 - kz + depth], axis=0)
                windows[g * group_rows : (g + 1) * group_rows, w * LANES : (w + 1) * LANES] = block.astype(
                    jnp.bfloat16
                )

    grads[...] = jnp.dot(xt[...], windows[...], preferred_element_type=jnp.float32)

    def blocks_of(tap, t):
        if tap >= TAPS:
            return jnp.zeros((8, LANES), jnp.float32)
        w, kx = tap // 3, tap % 3
        total = None
        for c_from in range(PACK):
            c = c_from + kx - 1
            block = c if 0 <= c < PACK else (PACK if c == PACK else 2 * PACK - 1)
            start = block * CH + t * 8
            value = grads[start : start + 8, w * LANES : (w + 1) * LANES]
            total = value if total is None else jnp.where(lane == c_from, value, total)
        return total

    near, even = lane < 2, lane % 2 == 0
    for half in range(2):
        for k in range(PACK):
            for t in range(PACK):
                sums = [blocks_of(PACK * (PACK * half + n) + k, t) for n in range(PACK)]
                first = jnp.where(near, sums[0], sums[2]) + pltpu.roll(jnp.where(near, sums[2], sums[0]), 64, 1)
                second = jnp.where(near, sums[1], sums[3]) + pltpu.roll(jnp.where(near, sums[3], sums[1]), 64, 1)
                other = jnp.where(even, second, first)
                packed = jnp.where(even, first, second) + jnp.where(
                    even, pltpu.roll(other, LANES - CH, 1), pltpu.roll(other, CH, 1)
                )
                place = 2 * ((half * PACK + k) * PACK + t)
                pieces[place] = packed[0:4]
                pieces[place + 1] = packed[4:8]

    def plane_copy(d, source, target):
        return pltpu.make_async_remote_copy(
            src_ref=source,
            dst_ref=target,
            send_sem=ring_send.at[0],
            recv_sem=ring_recv.at[0],
            device_id=plane_device(lax.rem(rank + d, n_plane)),
            device_id_type=MESH,
        )

    @pl.loop(1, n_plane)
    def _(d):
        plane_copy(d, pieces.at[lax.rem(rank + d, n_plane)], parts.at[n_plane - 1 - d]).start()

    wide_out = lax.dot_general(
        windows[...], bands[...], (((1,), (0,)), ((), ())), preferred_element_type=jnp.float32
    )
    own = wide_out[:, :LANES]
    outer = wide_out[:, LANES:]
    for g in range(groups):
        for layer in range(depth):

            def rows(value, group, layer=layer):
                start = (group % groups) * group_rows + layer * height
                return value[start : start + height]

            result = rows(own, g) + jnp.where(lane < PACK // 2, rows(outer, g - 1), rows(outer, g + 1))
            in_grad[layer, :, g * LANES : (g + 1) * LANES] = result.astype(jnp.bfloat16)

    def all_but_one(ref, sem):
        count = ref.shape[0] - 1
        return pltpu.make_async_copy(ref.at[pl.ds(0, count)], ref.at[pl.ds(0, count)], ring_recv.at[sem])

    pltpu.make_async_copy(parts, parts, ring_recv.at[0]).wait()
    total = pieces[rank]
    for k in range(n_plane - 1):
        total = total + parts[k]
    layers[z] = total

    @pl.loop(1, n_z)
    def _(d):
        pltpu.make_async_remote_copy(
            src_ref=layers.at[z],
            dst_ref=layers.at[z],
            send_sem=ring_send.at[1],
            recv_sem=ring_recv.at[1],
            device_id=z_device(lax.rem(z + d, n_z)),
            device_id_type=MESH,
        ).start()

    all_but_one(layers, 1).wait()
    total = layers[0]
    for k in range(1, n_z):
        total = total + layers[k]
    whole[rank] = total * scale

    @pl.loop(1, n_plane)
    def _(d):
        pltpu.make_async_remote_copy(
            src_ref=whole.at[rank],
            dst_ref=whole.at[rank],
            send_sem=ring_send.at[2],
            recv_sem=ring_recv.at[2],
            device_id=plane_device(lax.rem(rank + d, n_plane)),
            device_id_type=MESH,
        ).start()

    all_but_one(whole, 2).wait()
    for half in range(2):
        start = half * PIECES // 2
        block = jnp.concatenate([whole[start + k] for k in range(PIECES // 2)], axis=0).T
        for n in range(PACK):
            column = (half * PACK + n) * LANES
            count = min(LANES, f_v.shape[1] - column)
            if count > 0:
                filter_grad[:, column : column + count] = block[n * CH : (n + 1) * CH, :count]

    for send in sends:
        send.wait_send()
    pltpu.make_async_copy(parts, parts, ring_send.at[0]).wait()
    pltpu.make_async_copy(layers.at[pl.ds(0, n_z - 1)], layers.at[pl.ds(0, n_z - 1)], ring_send.at[1]).wait()
    pltpu.make_async_copy(parts, parts, ring_send.at[2]).wait()


def per_device(geometry, inputs, out_grad, filters):
    depth, height, width = inputs.shape
    filters = filters.T
    n_x, n_zlo, n_core, n_zhi, n_y = geometry
    n_plane, n_z = n_x * n_y * n_core, n_zhi * n_zlo
    groups = width // LANES
    rows = depth * height * groups
    bf16, f32 = jnp.bfloat16, jnp.float32
    scratch = [
        pltpu.VMEM((depth, height, width), bf16),
        pltpu.VMEM((depth, height, width), bf16),
        pltpu.VMEM(filters.shape, bf16),
        pltpu.VMEM((2 * depth, groups, LANES), f32),
        pltpu.VMEM((2 * depth, groups, LANES), bf16),
        pltpu.VMEM((height, width), bf16),
        pltpu.VMEM((height, width), bf16),
        pltpu.VMEM((2, depth + 2, groups, LANES), bf16),
        pltpu.VMEM((2, depth + 2, groups, LANES), f32),
        pltpu.VMEM((CH, LANES), f32),
        pltpu.VMEM((9 * LANES, 2 * LANES), bf16),
        pltpu.VMEM((2 * LANES, rows), bf16),
        pltpu.VMEM((rows, 9 * LANES), bf16),
        pltpu.VMEM((2 * LANES, 9 * LANES), f32),
        pltpu.VMEM((PIECES, 4, LANES), f32),
        pltpu.VMEM((n_plane - 1, 4, LANES), f32),
        pltpu.VMEM((n_z, 4, LANES), f32),
        pltpu.VMEM((n_plane, 4, LANES), f32),
        pltpu.SemaphoreType.DMA((3,)),
        pltpu.SemaphoreType.DMA((8,)),
        pltpu.SemaphoreType.DMA((8,)),
        pltpu.SemaphoreType.DMA((3,)),
        pltpu.SemaphoreType.DMA((3,)),
    ]
    cells = rows * PACK * n_plane * n_z
    scale = float(1.0 / (cells**0.5))
    in_grad, filter_grad = pl.pallas_call(
        functools.partial(kernel, geometry, scale),
        out_shape=(
            jax.ShapeDtypeStruct(inputs.shape, bf16),
            jax.ShapeDtypeStruct(filters.shape, f32),
        ),
        in_specs=[pl.BlockSpec(memory_space=pltpu.HBM)] * 3,
        out_specs=[pl.BlockSpec(memory_space=pltpu.VMEM)] * 2,
        scratch_shapes=scratch,
        compiler_params=pltpu.CompilerParams(
            collective_id=0, has_side_effects=True, vmem_limit_bytes=48 * 1024 * 1024
        ),
    )(inputs, out_grad, filters)
    return in_grad, filter_grad.T


def solution(mesh):
    n_gz, n_ch = mesh.shape["gz"], mesh.shape["ch"]
    n_zlo, n_core, n_zhi = 4, 2, 3
    geometry = (n_gz // (n_zlo * n_core), n_zlo, n_core, n_zhi, n_ch // n_zhi)
    placed = (P("gz", "ch", None), P("gz", "ch", None), P())
    return jax.shard_map(
        functools.partial(per_device, geometry),
        mesh=mesh,
        in_specs=placed,
        out_specs=(P("gz", "ch", None), P()),
        check_vma=False,
    )
```

time: 576 us -> 54.9 us (0.10)
  waiting for transfers between devices: 456 us -> 0 us
  local copies, waits for them, and re-layouts: 63.9 us -> 3.99 us
  Pallas kernels: 0 us -> 50 us
  starting transfers between devices: 28.9 us -> 0 us
  between operations: 14.6 us -> 0.65 us
  matrix products: 7.32 us -> 0 us
    psum x1 -> x0, waiting for transfers between devices: 456 us -> none  [per_device(): total = lax.psum(local_sum, ('gz', 'ch'))]
    pallas_call x0 -> x1, Pallas kernels: none -> 50 us  [per_device(): pl.pallas_call(functools.partial(kernel, geometry, scale), out_shape=(jax...]
    slice x15 -> x0, local copies, waits for them, and re-layouts: 31.7 us -> none  [the longest x10 28.6 us: per_device(): window = shifted[2 - kz:2 - kz + depth, 2 - ky:2 - ky + rows]]
    ppermute x4 -> x0, starting transfers between devices: 28.9 us -> none  [the longest x2 21.6 us: extended(): lax.ppermute(lax.slice_in_dim(block, 0, width, axis=dim), axis, backward)]
    reshape x48 -> x0, local copies, waits for them, and re-layouts: 26.8 us -> none  [the longest x9 19.1 us: per_device(): window = window.reshape(depth * rows * length, 3 * chans)]
    dot_general x18 -> x0, matrix products: 7.32 us -> none  [the longest x9 5.39 us: per_device(): lax.dot_general(values, window, (((0,), (0,)), ((), ())), preferred_eleme...]
  transfers between devices with their start and end apart: 5 -> 0, of which waited for: 1 -> 0; matrix products, arithmetic and copies ran while one was open for 2% -> 0% of each run, Pallas kernels for 0% -> 0%
where the time goes in v1:
time: 54.9 us; the launch traced here: 54.6 us
  Pallas kernels  50 us (91%)
  local copies, waits for them, and re-layouts  3.99 us (7%)
  between operations  0.65 us (1%)
    pallas_call x1, Pallas kernels, per_device(): pl.pallas_call(functools.partial(kernel, geometry, scale), out_shape=(jax...  50 us
    unnamed x8, local copies, waits for them, and re-layouts  3.99 us

profile of v1, /device:TPU:1, one launch (start us, length us, event | category | flops | bytes accessed | tf_op | source)
XLA Modules:
  0.0 54.6 jit_solution(17727277472902086597)
XLA Ops:
  0.6 0.0 copy-start
  0.6 0.9 %copy-done = bf16[2,8,6144]{2,1,0:T(8,128)(2,1)S(1)} copy-done((bf16[2,8,6144]{2,1,0:T(8,128)(2,1)S(1)}, bf16[2,8,6144]{2,1,0:T(8,128)(2,1)}, u32[]{:S(2)}) %copy-start) | copy-done | bytes 196632
  1.6 0.0 copy-start.1
  1.6 0.9 %copy-done.1 = bf16[2,8,6144]{2,1,0:T(8,128)(2,1)S(1)} copy-done((bf16[2,8,6144]{2,1,0:T(8,128)(2,1)S(1)}, bf16[2,8,6144]{2,1,0:T(8,128)(2,1)}, u32[]{:S(2)}) %copy-start.1) | copy-done | bytes 196632
  2.5 0.0 copy-start.2
  2.5 0.8 %copy-done.2 = bf16[864,32]{0,1:T(8,128)(2,1)S(1)} copy-done((bf16[864,32]{0,1:T(8,128)(2,1)S(1)}, bf16[864,32]{0,1:T(8,128)(2,1)}, u32[]{:S(2)}) %copy-start.2) | copy-done | bytes 55320
  3.3 50.0 %shard_map.50 = (bf16[2,8,6144]{2,1,0:T(8,128)(2,1)S(1)}, f32[32,864]{1,0:T(8,128)S(1)}) custom-call(bf16[2,8,6144]{2,1,0:T(8,128)(2,1)S(1)} %copy-done, bf16[2,8,6144]{2,1,0:T(8,128)(2,1)S(1)} %copy-done.1, bf16[32,864]{1,0:T(8,128)(2,1)S(1)} %bitcast.3), custom_call_target="tpu_custom_call" | custom-call | tf_op jit(solution)/shard_map/pallas_call | solution.py:357
  53.3 0.7 %copy.7 = bf16[2,8,6144]{2,1,0:T(8,128)(2,1)} copy(bf16[2,8,6144]{2,1,0:T(8,128)(2,1)S(1)} %get-tuple-element.8) | data formatting | bytes 393216
  54.0 0.6 %copy.8 = f32[864,32]{0,1:T(8,128)} copy(f32[864,32]{0,1:T(8,128)S(1)} %bitcast.2) | data formatting | bytes 221184
Async XLA Ops:
  0.6 0.9 %copy-start = (bf16[2,8,6144]{2,1,0:T(8,128)(2,1)S(1)}, bf16[2,8,6144]{2,1,0:T(8,128)(2,1)}, u32[]{:S(2)}) copy-start(bf16[2,8,6144]{2,1,0:T(8,128)(2,1)} %x_hbm.1) | copy-start | bytes 589828
  1.6 0.9 %copy-start.1 = (bf16[2,8,6144]{2,1,0:T(8,128)(2,1)S(1)}, bf16[2,8,6144]{2,1,0:T(8,128)(2,1)}, u32[]{:S(2)}) copy-start(bf16[2,8,6144]{2,1,0:T(8,128)(2,1)} %og_hbm.1) | copy-start | bytes 589828
  2.5 0.8 %copy-start.2 = (bf16[864,32]{0,1:T(8,128)(2,1)S(1)}, bf16[864,32]{0,1:T(8,128)(2,1)}, u32[]{:S(2)}) copy-start(bf16[864,32]{0,1:T(8,128)(2,1)} %param.5) | copy-start | bytes 165892

commit v2 on v1

--- a/solution.py
+++ b/solution.py
@@ -62,12 +62,39 @@
     rank = (x * n_y + y) * n_core + core
     z = z_hi * n_zlo + z_lo
 
-    def plane_device(r):
-        r_core, r_y, r_x = lax.rem(r, n_core), lax.rem(r // n_core, n_y), r // (n_core * n_y)
-        return ((r_x * n_zlo + z_lo) * n_core + r_core, z_hi * n_y + r_y)
-
-    def z_device(r):
-        return ((x * n_zlo + lax.rem(r, n_zlo)) * n_core + core, (r // n_zlo) * n_y + y)
+    def ways(size):
+        return sorted(range(size), key=lambda move: -min(move, size - move))
+
+    def moved(place, move, size):
+        return place if move == 0 else lax.rem(place + move, size)
+
+    x_at = [moved(x, move, n_x) for move in range(n_x)]
+    core_at = [moved(core, move, n_core) for move in range(n_core)]
+    near_moves = [(mx, mc) for mx in ways(n_x) for mc in ways(n_core)]
+
+    def plane_walk(act):
+        def row(my, there, alone):
+            for mx, mc in near_moves:
+                if alone and mx == 0 and mc == 0:
+                    continue
+                gz_there = (x_at[mx] * n_zlo + z_lo) * n_core + core_at[mc]
+                rank_there = (x_at[mx] * n_y + there) * n_core + core_at[mc]
+                act((gz_there, z_hi * n_y + there), rank_there, my * (n_x * n_core) + mx * n_core + mc - 1)
+
+        half = n_y // 2
+        row(half, lax.rem(y + half, n_y), False)
+
+        @pl.loop(1, half)
+        def _(j):
+            row(half + j, lax.rem(y + half + j, n_y), False)
+            row(half - j, lax.rem(y + half - j, n_y), False)
+
+        row(0, y, True)
+
+    z_moves = [(mh, ml) for mh in ways(n_zhi) for ml in ways(n_zlo) if mh or ml]
+    z_peers = [
+        ((x * n_zlo + moved(z_lo, ml, n_zlo)) * n_core + core, moved(z_hi, mh, n_zhi) * n_y + y) for mh, ml in z_moves
+    ]
 
     up, down = lax.rem(gz + 1, n_gz), lax.rem(gz + n_gz - 1, n_gz)
     right, left = lax.rem(ch + 1, n_ch), lax.rem(ch + n_ch - 1, n_ch)
@@ -85,15 +112,12 @@
     for device in neighbours:
         pl.semaphore_signal(barrier, inc=1, device_id=device, device_id_type=MESH)
 
-    @pl.loop(1, n_z)
-    def _(d):
-        pl.semaphore_signal(barrier, inc=1, device_id=z_device(lax.rem(z + d, n_z)), device_id_type=MESH)
-
-    @pl.loop(1, n_plane)
-    def _(d):
-        pl.semaphore_signal(
-            barrier, inc=1, device_id=plane_device(lax.rem(rank + d, n_plane)), device_id_type=MESH
-        )
+    def greet(device, *_):
+        pl.semaphore_signal(barrier, inc=1, device_id=device, device_id_type=MESH)
+
+    plane_walk(greet)
+    for device in z_peers:
+        greet(device)
 
     lane = lax.broadcasted_iota(jnp.int32, (height, LANES), 1) // CH
     row = lax.broadcasted_iota(jnp.int32, (height, LANES), 0)
@@ -110,6 +134,30 @@
     for k in range(2 * depth):
         edge[k] = rows32[k].astype(jnp.bfloat16)
 
+    pl.semaphore_wait(barrier, len(neighbours) + (n_z - 1) + (n_plane - 1))
+
+    halo = [
+        (edge.at[pl.ds(depth, depth)], y_side.at[0, pl.ds(1, depth)]),
+        (edge.at[pl.ds(0, depth)], y_side.at[1, pl.ds(1, depth)]),
+        (edge.at[depth + depth - 1], y_side.at[0, 0]),
+        (edge.at[depth], y_side.at[0, depth + 1]),
+        (edge.at[depth - 1], y_side.at[1, 0]),
+        (edge.at[0], y_side.at[1, depth + 1]),
+    ]
+    halo = [(og_v.at[depth - 1], z_low), (og_v.at[0], z_high)] + halo
+    sends = [
+        pltpu.make_async_remote_copy(
+            src_ref=source,
+            dst_ref=target,
+            send_sem=halo_send.at[k],
+            recv_sem=halo_recv.at[k],
+            device_id=neighbours[k],
+            device_id_type=MESH,
+        )
+        for k, (source, target) in enumerate(halo)
+    ]
+    for k in (4, 5, 6, 7, 2, 3, 0, 1):
+        sends[k].start()
     loads[2].wait()
     wide = lax.broadcasted_iota(jnp.int32, (CH, LANES), 1) // CH
     last = f_v.shape[1] // LANES
@@ -155,30 +203,6 @@
         xt[0:LANES, columns] = own.T.astype(jnp.bfloat16)
         xt[LANES : 2 * LANES, columns] = outer.T.astype(jnp.bfloat16)
 
-    pl.semaphore_wait(barrier, len(neighbours) + (n_z - 1) + (n_plane - 1))
-
-    halo = [
-        (edge.at[pl.ds(depth, depth)], y_side.at[0, pl.ds(1, depth)]),
-        (edge.at[pl.ds(0, depth)], y_side.at[1, pl.ds(1, depth)]),
-        (edge.at[depth + depth - 1], y_side.at[0, 0]),
-        (edge.at[depth], y_side.at[0, depth + 1]),
-        (edge.at[depth - 1], y_side.at[1, 0]),
-        (edge.at[0], y_side.at[1, depth + 1]),
-    ]
-    halo = [(og_v.at[depth - 1], z_low), (og_v.at[0], z_high)] + halo
-    sends = [
-        pltpu.make_async_remote_copy(
-            src_ref=source,
-            dst_ref=target,
-            send_sem=halo_send.at[k],
-            recv_sem=halo_recv.at[k],
-            device_id=neighbours[k],
-            device_id_type=MESH,
-        )
-        for k, (source, target) in enumerate(halo)
-    ]
-    for k in (4, 5, 6, 7, 2, 3, 0, 1):
-        sends[k].start()
     for send in sends:
         send.wait_recv()
 
@@ -191,16 +215,16 @@
         planes = [z_low[:, cut].astype(jnp.float32)]
         planes += [tile(og_v, layer, g) for layer in range(depth)]
         planes += [z_high[:, cut].astype(jnp.float32)]
-        moved = [[], planes, []]
+        turned = [[], planes, []]
         for layer, plane in enumerate(planes):
             low = jnp.broadcast_to(y_side32[0, layer, g : g + 1, :], plane.shape)
             high = jnp.broadcast_to(y_side32[1, layer, g : g + 1, :], plane.shape)
-            moved[2].append(jnp.where(row == 0, low, pltpu.roll(plane, 1, 0)))
-            moved[0].append(jnp.where(row == height - 1, high, pltpu.roll(plane, height - 1, 0)))
+            turned[2].append(jnp.where(row == 0, low, pltpu.roll(plane, 1, 0)))
+            turned[0].append(jnp.where(row == height - 1, high, pltpu.roll(plane, height - 1, 0)))
         for kz in range(3):
             for ky in range(3):
                 w = 3 * kz + ky
-                block = jnp.concatenate(moved[ky][2 - kz : 2 - kz + depth], axis=0)
+                block = jnp.concatenate(turned[ky][2 - kz : 2 - kz + depth], axis=0)
                 windows[g * group_rows : (g + 1) * group_rows, w * LANES : (w + 1) * LANES] = block.astype(
                     jnp.bfloat16
                 )
@@ -235,19 +259,17 @@
                 pieces[place] = packed[0:4]
                 pieces[place + 1] = packed[4:8]
 
-    def plane_copy(d, source, target):
-        return pltpu.make_async_remote_copy(
-            src_ref=source,
-            dst_ref=target,
+    def send_part(device, rank_there, offset):
+        pltpu.make_async_remote_copy(
+            src_ref=pieces.at[rank_there],
+            dst_ref=parts.at[offset],
             send_sem=ring_send.at[0],
             recv_sem=ring_recv.at[0],
-            device_id=plane_device(lax.rem(rank + d, n_plane)),
+            device_id=device,
             device_id_type=MESH,
-        )
-
-    @pl.loop(1, n_plane)
-    def _(d):
-        plane_copy(d, pieces.at[lax.rem(rank + d, n_plane)], parts.at[n_plane - 1 - d]).start()
+        ).start()
+
+    plane_walk(send_part)
 
     wide_out = lax.dot_general(
         windows[...], bands[...], (((1,), (0,)), ((), ())), preferred_element_type=jnp.float32
@@ -274,14 +296,13 @@
         total = total + parts[k]
     layers[z] = total
 
-    @pl.loop(1, n_z)
-    def _(d):
+    for device in z_peers:
         pltpu.make_async_remote_copy(
             src_ref=layers.at[z],
             dst_ref=layers.at[z],
             send_sem=ring_send.at[1],
             recv_sem=ring_recv.at[1],
-            device_id=z_device(lax.rem(z + d, n_z)),
+            device_id=device,
             device_id_type=MESH,
         ).start()
 
@@ -291,16 +312,17 @@
         total = total + layers[k]
     whole[rank] = total * scale
 
-    @pl.loop(1, n_plane)
-    def _(d):
+    def send_whole(device, *_):
         pltpu.make_async_remote_copy(
             src_ref=whole.at[rank],
             dst_ref=whole.at[rank],
             send_sem=ring_send.at[2],
             recv_sem=ring_recv.at[2],
-            device_id=plane_device(lax.rem(rank + d, n_plane)),
+            device_id=device,
             device_id_type=MESH,
         ).start()
+
+    plane_walk(send_whole)
 
     all_but_one(whole, 2).wait()
     for half in range(2):
@@ -366,7 +388,7 @@
         compiler_params=pltpu.CompilerParams(
             collective_id=0, has_side_effects=True, vmem_limit_bytes=48 * 1024 * 1024
         ),
-    )(inputs, out_grad, filters)
+    )(*(pltpu.with_memory_space_constraint(value, pltpu.HBM) for value in (inputs, out_grad, filters)))
     return in_grad, filter_grad.T
 
 

time: 54.9 us -> 50 us (0.911)
  local copies, waits for them, and re-layouts: 3.99 us -> 1.32 us
  Pallas kernels: 50 us -> 47.9 us
    unnamed x8 -> x2, local copies, waits for them, and re-layouts: 3.99 us -> 1.32 us
    pallas_call x1, Pallas kernels: 50 us -> 47.9 us  [per_device(): pl.pallas_call(functools.partial(kernel, geometry, scale), out_shape=(jax...]
where the time goes in v2:
time: 50 us; the launch traced here: 49.9 us
  Pallas kernels  47.9 us (96%)
  local copies, waits for them, and re-layouts  1.32 us (3%)
  between operations  0.64 us (1%)
    pallas_call x1, Pallas kernels, per_device(): pl.pallas_call(functools.partial(kernel, geometry, scale), out_shape=(jax...  47.9 us
    unnamed x2, local copies, waits for them, and re-layouts  1.32 us

profile of v2, /device:TPU:1, one launch (start us, length us, event | category | flops | bytes accessed | tf_op | source)
XLA Modules:
  0.0 49.9 jit_solution(15964174847098288542)
XLA Ops:
  0.6 47.9 %shard_map.50 = (bf16[2,8,6144]{2,1,0:T(8,128)(2,1)S(1)}, f32[32,864]{1,0:T(8,128)S(1)}) custom-call(bf16[2,8,6144]{2,1,0:T(8,128)(2,1)} %x_hbm.1, bf16[2,8,6144]{2,1,0:T(8,128)(2,1)} %og_hbm.1, bf16[32,864]{1,0:T(8,128)(2,1)} %bitcast.3), custom_call_target="tpu_custom_call" | custom-call | tf_op jit(solution)/shard_map/pallas_call | solution.py:379
  48.6 0.7 %copy.7 = bf16[2,8,6144]{2,1,0:T(8,128)(2,1)} copy(bf16[2,8,6144]{2,1,0:T(8,128)(2,1)S(1)} %get-tuple-element.8) | data formatting | bytes 393216
  49.2 0.6 %copy.8 = f32[864,32]{0,1:T(8,128)} copy(f32[864,32]{0,1:T(8,128)S(1)} %bitcast.2) | data formatting | bytes 221184

commit v3 on v2

--- a/solution.py
+++ b/solution.py
@@ -341,6 +341,17 @@
     pltpu.make_async_copy(parts, parts, ring_send.at[2]).wait()
 
 
+def put_out(in_grad_v, filter_grad_v, in_grad, filter_grad, sems):
+    copies = [
+        pltpu.make_async_copy(filter_grad_v, filter_grad, sems.at[0]),
+        pltpu.make_async_copy(in_grad_v, in_grad, sems.at[1]),
+    ]
+    for copy in copies:
+        copy.start()
+    for copy in copies:
+        copy.wait()
+
+
 def per_device(geometry, inputs, out_grad, filters):
     depth, height, width = inputs.shape
     filters = filters.T
@@ -389,6 +400,17 @@
             collective_id=0, has_side_effects=True, vmem_limit_bytes=48 * 1024 * 1024
         ),
     )(*(pltpu.with_memory_space_constraint(value, pltpu.HBM) for value in (inputs, out_grad, filters)))
+    in_grad, filter_grad = pl.pallas_call(
+        put_out,
+        out_shape=(
+            jax.ShapeDtypeStruct(in_grad.shape, bf16),
+            jax.ShapeDtypeStruct(filter_grad.shape, f32),
+        ),
+        in_specs=[pl.BlockSpec(memory_space=pltpu.VMEM)] * 2,
+        out_specs=[pl.BlockSpec(memory_space=pltpu.HBM)] * 2,
+        scratch_shapes=[pltpu.SemaphoreType.DMA((2,))],
+        compiler_params=pltpu.CompilerParams(vmem_limit_bytes=8 * 1024 * 1024),
+    )(in_grad, filter_grad)
     return in_grad, filter_grad.T
 
 

time: 50 us -> 49.4 us (0.988)
  local copies, waits for them, and re-layouts: 1.32 us -> 0 us
  Pallas kernels: 47.9 us -> 48.7 us
    unnamed x2 -> x0, local copies, waits for them, and re-layouts: 1.32 us -> none
    pallas_call x0 -> x1, Pallas kernels: none -> 0.73 us  [per_device(): pl.pallas_call(put_out, out_shape=(jax.ShapeDtypeStruct(in_grad.shape, bf...]
where the time goes in v3:
time: 49.4 us; the launch traced here: 49.3 us
  Pallas kernels  48.7 us (99%)
  between operations  0.64 us (1%)
    pallas_call x1, Pallas kernels, per_device(): pl.pallas_call(functools.partial(kernel, geometry, scale), out_shape=(jax...  47.9 us

profile of v3, /device:TPU:1, one launch (start us, length us, event | category | flops | bytes accessed | tf_op | source)
XLA Modules:
  0.0 49.3 jit_solution(7249681428288742448)
XLA Ops:
  0.6 47.9 %shard_map.50 = (bf16[2,8,6144]{2,1,0:T(8,128)(2,1)S(1)}, f32[32,864]{1,0:T(8,128)S(1)}) custom-call(bf16[2,8,6144]{2,1,0:T(8,128)(2,1)} %x_hbm.1, bf16[2,8,6144]{2,1,0:T(8,128)(2,1)} %og_hbm.1, bf16[32,864]{1,0:T(8,128)(2,1)} %bitcast.2), custom_call_target="tpu_custom_call" | custom-call | tf_op jit(solution)/shard_map/pallas_call | solution.py:390
  48.6 0.7 %shard_map.51 = (bf16[2,8,6144]{2,1,0:T(8,128)(2,1)}, f32[32,864]{1,0:T(8,128)}) custom-call(bf16[2,8,6144]{2,1,0:T(8,128)(2,1)S(1)} %get-tuple-element.6.in_grad_v, f32[32,864]{1,0:T(8,128)S(1)} %get-tuple-element.7.filter_grad_v), custom_call_target="tpu_custom_call" | custom-call | tf_op jit(solution)/shard_map/pallas_call | solution.py:403

commit v4 on v3

--- a/solution.py
+++ b/solution.py
@@ -11,7 +11,7 @@
 CH = 32
 LANES = 128
 PACK = LANES // CH
-PIECES = 64
+PIECES = 32
 TAPS = 27
 
 
@@ -91,6 +91,11 @@
 
         row(0, y, True)
 
+    owner_rows = [(n_y - 2 + k) % n_y for k in range(4)]
+    own_row = lax.rem(y + 2, n_y)
+    owner = own_row < len(owner_rows)
+    mine = (x * len(owner_rows) + lax.rem(own_row, len(owner_rows))) * n_core + core
+
     z_moves = [(mh, ml) for mh in ways(n_zhi) for ml in ways(n_zlo) if mh or ml]
     z_peers = [
         ((x * n_zlo + moved(z_lo, ml, n_zlo)) * n_core + core, moved(z_hi, mh, n_zhi) * n_y + y) for mh, ml in z_moves
@@ -203,7 +208,23 @@
         xt[0:LANES, columns] = own.T.astype(jnp.bfloat16)
         xt[LANES : 2 * LANES, columns] = outer.T.astype(jnp.bfloat16)
 
-    for send in sends:
+    def planes_of(g):
+        cut = slice(g * LANES, (g + 1) * LANES)
+        planes = [z_low[:, cut].astype(jnp.float32)]
+        planes += [tile(og_v, layer, g) for layer in range(depth)]
+        return planes + [z_high[:, cut].astype(jnp.float32)]
+
+    def put_window(g, ky, planes):
+        for kz in range(3):
+            w = 3 * kz + ky
+            block = jnp.concatenate(planes[2 - kz : 2 - kz + depth], axis=0)
+            windows[g * group_rows : (g + 1) * group_rows, w * LANES : (w + 1) * LANES] = block.astype(jnp.bfloat16)
+
+    for send in sends[:2]:
+        send.wait_recv()
+    for g in range(groups):
+        put_window(g, 1, planes_of(g))
+    for send in sends[2:]:
         send.wait_recv()
 
     for side in range(2):
@@ -211,23 +232,14 @@
             y_side32[side, layer] = y_side[side, layer].astype(jnp.float32)
 
     for g in range(groups):
-        cut = slice(g * LANES, (g + 1) * LANES)
-        planes = [z_low[:, cut].astype(jnp.float32)]
-        planes += [tile(og_v, layer, g) for layer in range(depth)]
-        planes += [z_high[:, cut].astype(jnp.float32)]
-        turned = [[], planes, []]
-        for layer, plane in enumerate(planes):
+        before, after = [], []
+        for layer, plane in enumerate(planes_of(g)):
             low = jnp.broadcast_to(y_side32[0, layer, g : g + 1, :], plane.shape)
             high = jnp.broadcast_to(y_side32[1, layer, g : g + 1, :], plane.shape)
-            turned[2].append(jnp.where(row == 0, low, pltpu.roll(plane, 1, 0)))
-            turned[0].append(jnp.where(row == height - 1, high, pltpu.roll(plane, height - 1, 0)))
-        for kz in range(3):
-            for ky in range(3):
-                w = 3 * kz + ky
-                block = jnp.concatenate(turned[ky][2 - kz : 2 - kz + depth], axis=0)
-                windows[g * group_rows : (g + 1) * group_rows, w * LANES : (w + 1) * LANES] = block.astype(
-                    jnp.bfloat16
-                )
+            before.append(jnp.where(row == height - 1, high, pltpu.roll(plane, height - 1, 0)))
+            after.append(jnp.where(row == 0, low, pltpu.roll(plane, 1, 0)))
+        put_window(g, 0, before)
+        put_window(g, 2, after)
 
     grads[...] = jnp.dot(xt[...], windows[...], preferred_element_type=jnp.float32)
 
@@ -255,21 +267,25 @@
                 packed = jnp.where(even, first, second) + jnp.where(
                     even, pltpu.roll(other, LANES - CH, 1), pltpu.roll(other, CH, 1)
                 )
-                place = 2 * ((half * PACK + k) * PACK + t)
-                pieces[place] = packed[0:4]
-                pieces[place + 1] = packed[4:8]
-
-    def send_part(device, rank_there, offset):
-        pltpu.make_async_remote_copy(
-            src_ref=pieces.at[rank_there],
-            dst_ref=parts.at[offset],
-            send_sem=ring_send.at[0],
-            recv_sem=ring_recv.at[0],
-            device_id=device,
-            device_id_type=MESH,
-        ).start()
-
-    plane_walk(send_part)
+                pieces[(half * PACK + k) * PACK + t] = packed
+
+    for mx, mc in near_moves:
+        for k, there in enumerate(owner_rows):
+
+            def send_part(mx=mx, mc=mc, k=k, there=there):
+                pltpu.make_async_remote_copy(
+                    src_ref=pieces.at[(x_at[mx] * len(owner_rows) + k) * n_core + core_at[mc]],
+                    dst_ref=parts.at[y * (n_x * n_core) + mx * n_core + mc],
+                    send_sem=ring_send.at[0],
+                    recv_sem=ring_recv.at[0],
+                    device_id=((x_at[mx] * n_zlo + z_lo) * n_core + core_at[mc], z_hi * n_y + there),
+                    device_id_type=MESH,
+                ).start()
+
+            if mx == 0 and mc == 0:
+                pl.when(y != there)(send_part)
+            else:
+                send_part()
 
     wide_out = lax.dot_general(
         windows[...], bands[...], (((1,), (0,)), ((), ())), preferred_element_type=jnp.float32
@@ -290,41 +306,56 @@
         count = ref.shape[0] - 1
         return pltpu.make_async_copy(ref.at[pl.ds(0, count)], ref.at[pl.ds(0, count)], ring_recv.at[sem])
 
-    pltpu.make_async_copy(parts, parts, ring_recv.at[0]).wait()
-    total = pieces[rank]
-    for k in range(n_plane - 1):
-        total = total + parts[k]
-    layers[z] = total
-
-    for device in z_peers:
-        pltpu.make_async_remote_copy(
-            src_ref=layers.at[z],
-            dst_ref=layers.at[z],
-            send_sem=ring_send.at[1],
-            recv_sem=ring_recv.at[1],
-            device_id=device,
-            device_id_type=MESH,
-        ).start()
-
-    all_but_one(layers, 1).wait()
-    total = layers[0]
-    for k in range(1, n_z):
-        total = total + layers[k]
-    whole[rank] = total * scale
-
-    def send_whole(device, *_):
-        pltpu.make_async_remote_copy(
-            src_ref=whole.at[rank],
-            dst_ref=whole.at[rank],
-            send_sem=ring_send.at[2],
-            recv_sem=ring_recv.at[2],
-            device_id=device,
-            device_id_type=MESH,
-        ).start()
-
-    plane_walk(send_whole)
-
-    all_but_one(whole, 2).wait()
+    def spent(ref, count, sem):
+        return pltpu.make_async_copy(ref.at[pl.ds(0, count)], ref.at[pl.ds(0, count)], sem)
+
+    @pl.when(owner)
+    def _():
+        parts[y * (n_x * n_core)] = pieces[mine]
+        all_but_one(parts, 0).wait()
+        total = parts[0]
+        for k in range(1, n_plane):
+            total = total + parts[k]
+        layers[z] = total
+        for device in z_peers:
+            pltpu.make_async_remote_copy(
+                src_ref=layers.at[z],
+                dst_ref=layers.at[z],
+                send_sem=ring_send.at[1],
+                recv_sem=ring_recv.at[1],
+                device_id=device,
+                device_id_type=MESH,
+            ).start()
+        all_but_one(layers, 1).wait()
+        total = layers[0]
+        for k in range(1, n_z):
+            total = total + layers[k]
+        whole[mine] = total * scale
+
+        for there in sorted(range(n_y), key=lambda line: min(line, n_y - line)):
+            for mx, mc in near_moves:
+
+                def send_whole(mx=mx, mc=mc, there=there):
+                    pltpu.make_async_remote_copy(
+                        src_ref=whole.at[mine],
+                        dst_ref=whole.at[mine],
+                        send_sem=ring_send.at[2],
+                        recv_sem=ring_recv.at[2],
+                        device_id=((x_at[mx] * n_zlo + z_lo) * n_core + core_at[mc], z_hi * n_y + there),
+                        device_id_type=MESH,
+                    ).start()
+
+                if mx == 0 and mc == 0:
+                    pl.when(y != there)(send_whole)
+                else:
+                    send_whole()
+
+        all_but_one(whole, 2).wait()
+
+    @pl.when(jnp.logical_not(owner))
+    def _():
+        spent(whole, PIECES, ring_recv.at[2]).wait()
+
     for half in range(2):
         start = half * PIECES // 2
         block = jnp.concatenate([whole[start + k] for k in range(PIECES // 2)], axis=0).T
@@ -336,9 +367,15 @@
 
     for send in sends:
         send.wait_send()
-    pltpu.make_async_copy(parts, parts, ring_send.at[0]).wait()
-    pltpu.make_async_copy(layers.at[pl.ds(0, n_z - 1)], layers.at[pl.ds(0, n_z - 1)], ring_send.at[1]).wait()
-    pltpu.make_async_copy(parts, parts, ring_send.at[2]).wait()
+    @pl.when(owner)
+    def _():
+        spent(pieces, PIECES - 1, ring_send.at[0]).wait()
+        spent(layers, n_z - 1, ring_send.at[1]).wait()
+        spent(parts, n_plane - 1, ring_send.at[2]).wait()
+
+    @pl.when(jnp.logical_not(owner))
+    def _():
+        spent(pieces, PIECES, ring_send.at[0]).wait()
 
 
 def put_out(in_grad_v, filter_grad_v, in_grad, filter_grad, sems):
@@ -375,10 +412,10 @@
         pltpu.VMEM((2 * LANES, rows), bf16),
         pltpu.VMEM((rows, 9 * LANES), bf16),
         pltpu.VMEM((2 * LANES, 9 * LANES), f32),
-        pltpu.VMEM((PIECES, 4, LANES), f32),
-        pltpu.VMEM((n_plane - 1, 4, LANES), f32),
-        pltpu.VMEM((n_z, 4, LANES), f32),
-        pltpu.VMEM((n_plane, 4, LANES), f32),
+        pltpu.VMEM((PIECES, 8, LANES), f32),
+        pltpu.VMEM((n_plane, 8, LANES), f32),
+        pltpu.VMEM((n_z, 8, LANES), f32),
+        pltpu.VMEM((PIECES, 8, LANES), f32),
         pltpu.SemaphoreType.DMA((3,)),
         pltpu.SemaphoreType.DMA((8,)),
         pltpu.SemaphoreType.DMA((8,)),

time: 49.4 us -> 49.1 us (level)
  the two profiles are of different devices: /device:TPU:1 before, /device:TPU:33 now
where the time goes in v4:
time: 49.1 us; the launch traced here: 48.9 us
  Pallas kernels  48.3 us (98%)
  between operations  0.64 us (1%)
    pallas_call x1, Pallas kernels, per_device(): pl.pallas_call(functools.partial(kernel, geometry, scale), out_shape=(jax...  47.5 us

profile of v4, /device:TPU:33, one launch (start us, length us, event | category | flops | bytes accessed | tf_op | source)
XLA Modules:
  0.0 48.9 jit_solution(3411758550200031228)
XLA Ops:
  0.6 47.5 %shard_map.50 = (bf16[2,8,6144]{2,1,0:T(8,128)(2,1)S(1)}, f32[32,864]{1,0:T(8,128)S(1)}) custom-call(bf16[2,8,6144]{2,1,0:T(8,128)(2,1)} %x_hbm.1, bf16[2,8,6144]{2,1,0:T(8,128)(2,1)} %og_hbm.1, bf16[32,864]{1,0:T(8,128)(2,1)} %bitcast.2), custom_call_target="tpu_custom_call" | custom-call | tf_op jit(solution)/shard_map/pallas_call | solution.py:427
  48.2 0.7 %shard_map.51 = (bf16[2,8,6144]{2,1,0:T(8,128)(2,1)}, f32[32,864]{1,0:T(8,128)}) custom-call(bf16[2,8,6144]{2,1,0:T(8,128)(2,1)S(1)} %get-tuple-element.6.in_grad_v, f32[32,864]{1,0:T(8,128)S(1)} %get-tuple-element.7.filter_grad_v), custom_call_target="tpu_custom_call" | custom-call | tf_op jit(solution)/shard_map/pallas_call | solution.py:440

commit v5 on v3

--- a/solution.py
+++ b/solution.py
@@ -115,9 +115,9 @@
     def greet(device, *_):
         pl.semaphore_signal(barrier, inc=1, device_id=device, device_id_type=MESH)
 
-    plane_walk(greet)
     for device in z_peers:
         greet(device)
+    plane_walk(greet)
 
     lane = lax.broadcasted_iota(jnp.int32, (height, LANES), 1) // CH
     row = lax.broadcasted_iota(jnp.int32, (height, LANES), 0)

time: 49.4 us -> 49.3 us (level)
  no operation moved by 1% of the time
where the time goes in v5:
time: 49.3 us; the launch traced here: 49.2 us
  Pallas kernels  48.5 us (98%)
  between operations  0.64 us (1%)
    pallas_call x1, Pallas kernels, per_device(): pl.pallas_call(functools.partial(kernel, geometry, scale), out_shape=(jax...  47.8 us

profile of v5, /device:TPU:1, one launch (start us, length us, event | category | flops | bytes accessed | tf_op | source)
XLA Modules:
  0.0 49.2 jit_solution(9755740797523198250)
XLA Ops:
  0.6 47.8 %shard_map.50 = (bf16[2,8,6144]{2,1,0:T(8,128)(2,1)S(1)}, f32[32,864]{1,0:T(8,128)S(1)}) custom-call(bf16[2,8,6144]{2,1,0:T(8,128)(2,1)} %x_hbm.1, bf16[2,8,6144]{2,1,0:T(8,128)(2,1)} %og_hbm.1, bf16[32,864]{1,0:T(8,128)(2,1)} %bitcast.2), custom_call_target="tpu_custom_call" | custom-call | tf_op jit(solution)/shard_map/pallas_call | solution.py:390
  48.4 0.7 %shard_map.51 = (bf16[2,8,6144]{2,1,0:T(8,128)(2,1)}, f32[32,864]{1,0:T(8,128)}) custom-call(bf16[2,8,6144]{2,1,0:T(8,128)(2,1)S(1)} %get-tuple-element.6.in_grad_v, f32[32,864]{1,0:T(8,128)S(1)} %get-tuple-element.7.filter_grad_v), custom_call_target="tpu_custom_call" | custom-call | tf_op jit(solution)/shard_map/pallas_call | solution.py:403
